TPU v7x, 32 devices: a whole 2x2x4 slice. The times are simulated.
32 devices in a mesh: band: 4 (over x, core), slab: 8 (over z, y).
Axes of the slice: x: 2, y: 2, z: 4, core: 2. Of those that a mesh axis runs over, the one named last changes fastest.
Arguments:
- resident: float32 [8, 128, 128, 128], P('band', 'slab'), may hold values from -5 to 5
- blocks: float32 [16, 128, 128, 128], P('band', 'slab'), may hold values from -5 to 5
- occupation: float32 [16], replicated, may hold values from 0.25 to 1
Outputs:
- exchange_term: float32 [8, 128, 128, 128], P('band', 'slab')
All inputs are finite; a program needn't handle non-finite values.
Results may differ from a plain program's by a relative error of at most 0.0001.
Values sent between devices are 32-bit elements; how exact they have to be, the bound alone decides.
No kernel may reach another device: no remote copies, remote signals or barrier semaphores. Data moves between devices by JAX's collectives and lax.ppermute only.
A program may use at most 192 MiB of HBM per device.

v0:
```python
import math

import jax
import jax.numpy as jnp
from jax import lax
from jax.sharding import PartitionSpec as P

KAPPA_SQ = 0.01


def dft_tables(grid_len):
    indices = jnp.arange(grid_len, dtype=jnp.int32)
    product = indices[:, None] * indices[None, :] % grid_len
    angles = product.astype(jnp.float32) * (2.0 * math.pi / grid_len)
    return (jnp.cos(angles), jnp.sin(angles))


def transform(real_part, imag_part, form, cos_t, sin_t, sign_val):

    def apply(values, table):
        return jnp.einsum(
            form, values, table, precision=lax.Precision.HIGHEST, preferred_element_type=jnp.float32
        )

    real_cos = apply(real_part, cos_t)
    real_sin = apply(real_part, sin_t)
    imag_cos = apply(imag_part, cos_t)
    imag_sin = apply(imag_part, sin_t)
    return (real_cos - sign_val * imag_sin, imag_cos + sign_val * real_sin)


def wave_of(indices, grid_len):
    signed = jnp.where(indices > (grid_len - 1) // 2, indices - grid_len, indices)
    return signed.astype(jnp.float32) * (2.0 * math.pi / grid_len)


def coulomb(wave_z, wave_y, wave_x):
    squared = wave_z[:, None, None] ** 2 + wave_y[None, :, None] ** 2 + wave_x[None, None, :] ** 2
    return 4.0 * math.pi / (squared + KAPPA_SQ)


def per_device(resident, blocks, occupation):
    orb_count, plane_count, grid_len, _ = resident.shape
    local_src = blocks.shape[0]
    group_count = lax.axis_size("band")
    src_count = local_src * group_count
    cos_t, sin_t = dft_tables(grid_len)
    along_x = "fzyx,xk->fzyk"
    along_y = "fzyx,yk->fzkx"
    along_z = "fzyx,zk->fkyx"
    source = lax.all_gather(blocks, "band", axis=0, tiled=True)
    count_pairs = source.shape[0] // 2
    even_src = source[0::2]
    odd_src = source[1::2]
    real_part = (resident[:, None] * even_src[None]).reshape(
        orb_count * count_pairs, plane_count, grid_len, grid_len
    )
    imag_part = (resident[:, None] * odd_src[None]).reshape(
        orb_count * count_pairs, plane_count, grid_len, grid_len
    )
    real_part, imag_part = transform(real_part, imag_part, along_x, cos_t, sin_t, -1.0)
    real_part, imag_part = transform(real_part, imag_part, along_y, cos_t, sin_t, -1.0)
    shaped = (orb_count, count_pairs, plane_count, grid_len, grid_len)
    real_part, imag_part = (real_part.reshape(shaped), imag_part.reshape(shaped))
    field_count = orb_count * (src_count // 2)
    flat = (field_count, plane_count, grid_len, grid_len)
    real_part = real_part.reshape(flat)
    imag_part = imag_part.reshape(flat)
    all_waves = wave_of(jnp.arange(grid_len, dtype=jnp.int32), grid_len)
    position = lax.axis_index("slab")
    col_real = lax.all_to_all(real_part, "slab", split_axis=2, concat_axis=1, tiled=True)
    col_imag = lax.all_to_all(imag_part, "slab", split_axis=2, concat_axis=1, tiled=True)
    width_y = col_real.shape[2]
    local_waves = wave_of(position * width_y + jnp.arange(width_y, dtype=jnp.int32), grid_len)
    kernel = coulomb(all_waves, local_waves, all_waves)
    col_real, col_imag = transform(col_real, col_imag, along_z, cos_t, sin_t, -1.0)
    col_real = col_real * kernel[None]
    col_imag = col_imag * kernel[None]
    col_real, col_imag = transform(col_real, col_imag, along_z, cos_t, sin_t, 1.0)
    real_part = lax.all_to_all(col_real, "slab", split_axis=1, concat_axis=2, tiled=True)
    imag_part = lax.all_to_all(col_imag, "slab", split_axis=1, concat_axis=2, tiled=True)
    real_part, imag_part = transform(real_part, imag_part, along_y, cos_t, sin_t, 1.0)
    real_part, imag_part = transform(real_part, imag_part, along_x, cos_t, sin_t, 1.0)
    scale_inv = 1.0 / float(grid_len * grid_len * grid_len)
    shaped = (orb_count, src_count // 2, plane_count, grid_len, grid_len)
    pot_even = real_part.reshape(shaped) * scale_inv
    pot_odd = imag_part.reshape(shaped) * scale_inv
    weighted_even = source[0::2] * occupation[0::2][:, None, None, None]
    weighted_odd = source[1::2] * occupation[1::2][:, None, None, None]
    summed = jnp.sum(pot_even * weighted_even[None], axis=1) + jnp.sum(
        pot_odd * weighted_odd[None], axis=1
    )
    return -summed


def solution(mesh):
    placed = (P("band", "slab", None, None), P("band", "slab", None, None), P())
    return jax.shard_map(
        per_device,
        mesh=mesh,
        in_specs=placed,
        out_specs=P("band", "slab", None, None),
        check_vma=False,
    )
```

profile of v0, /device:TPU:0, one launch (start us, length us, event | category | flops | bytes accessed | tf_op | source)
XLA Modules:
  0.0 2126.6 jit_solution(9752957282136945423)
XLA Ops:
  6.5 0.0 all-gather.2.cloned.1.call-start
  6.5 0.7 all-gather.2.cloned.1.call-update
  7.3 0.7 slice.17
  8.0 0.7 slice.16
  8.7 0.0 copy-start.2
  8.8 108.8 %all-gather.2.cloned.1.call-done = f32[16,16,128,128]{3,2,1,0:T(8,128)} async-done(((f32[4,16,128,128]{3,2,1,0:T(8,128)}), f32[16,16,128,128]{3,2,1,0:T(8,128)}) %all-gather.2.cloned.1.call-update) | async-done | bytes 16777232 | tf_op jit(solution)/shard_map/all_gather | solution.py:51
  117.5 15.9 multiply_multiply_fusion
  133.5 0.0 copy-done.2
  133.5 12.9 broadcast_multiply_fusion.1
  146.4 16.6 fusion.50
  163.0 18.9 fusion.52
  182.0 22.5 %multiply_add_fusion = f32[16,16,128,128]{3,2,1,0:T(8,128)} fusion(f32[16,16,128,128]{3,2,1,0:T(8,128)} %fusion.50, f32[16,16,128,128]{3,2,1,0:T(8,128)} %bitcast.155), kind=kOutput, calls=%fused_computation.24 | convolution fusion | flops 6451068928 | bytes 50331648 | tf_op jit(solution)/shard_map/fzyx,xk->fzyk/dot_general | solution.py:21
  204.4 18.9 multiply_subtract_fusion
  223.4 22.6 %fusion.54 = f32[128,16,16,128]{3,0,2,1:T(8,128)} fusion(f32[16,16,128,128]{3,2,1,0:T(8,128)} %multiply_subtract_fusion), kind=kOutput, calls=%fused_computation.67 | convolution fusion | flops 6442680320 | bytes 33554432 | tf_op jit(solution)/shard_map/fzyx,yk->fzkx/dot_general | solution.py:21
  245.9 25.8 %subtract_bitcast_fusion.1 = f32[16,16,128,128]{3,2,1,0:T(8,128)} fusion(f32[128,16,16,128]{3,0,2,1:T(8,128)} %fusion.54, f32[16,16,128,128]{3,2,1,0:T(8,128)} %multiply_add_fusion), kind=kOutput, calls=%fused_computation.23 | convolution fusion | flops 6451068928 | bytes 50331648 | tf_op jit(solution)/shard_map/fzyx,yk->fzkx/dot_general | solution.py:21
  271.7 17.8 copy.26
  289.4 6.0 all-to-all-start
  295.4 22.2 %fusion.46 = f32[128,16,16,128]{3,0,2,1:T(8,128)} fusion(f32[16,16,128,128]{3,2,1,0:T(8,128)} %multiply_add_fusion), kind=kOutput, calls=%fused_computation.59 | convolution fusion | flops 6442680320 | bytes 33554432 | tf_op jit(solution)/shard_map/fzyx,yk->fzkx/dot_general | solution.py:21
  317.6 26.1 %add_bitcast_fusion.1 = f32[16,16,128,128]{3,2,1,0:T(8,128)} fusion(f32[128,16,16,128]{3,0,2,1:T(8,128)} %fusion.46, f32[16,16,128,128]{3,2,1,0:T(8,128)} %multiply_subtract_fusion), kind=kOutput, calls=%fused_computation.22 | convolution fusion | flops 6451068928 | bytes 50331648 | tf_op jit(solution)/shard_map/fzyx,yk->fzkx/dot_general | solution.py:21
  343.7 17.7 copy.31
  361.5 297.4 %all-to-all-done = f32[16,16,128,128]{3,1,0,2:T(8,128)} async-done(((f32[16,16,128,128]{3,1,0,2:T(8,128)}), f32[16,16,128,128]{3,1,0,2:T(8,128)}, u32[]{:S(2)}, u32[]{:S(2)}) %all-to-all-start) | async-done | bytes 16777248 | tf_op jit(solution)/shard_map/all_to_all | solution.py:71
  658.9 5.9 all-to-all-start.1
  664.9 0.1 broadcast_add_fusion
  664.9 0.3 add_divide_fusion
  665.3 11.9 copy.27
  677.2 350.3 %all-to-all-done.1 = f32[16,16,128,128]{3,1,0,2:T(8,128)} async-done(((f32[16,16,128,128]{3,1,0,2:T(8,128)}), f32[16,16,128,128]{3,1,0,2:T(8,128)}, u32[]{:S(2)}, u32[]{:S(2)}) %all-to-all-start.1) | async-done | bytes 16777248 | tf_op jit(solution)/shard_map/all_to_all | solution.py:72
  1027.5 11.9 copy.32
  1039.4 22.1 %fusion.44 = f32[128,16,16,128]{3,0,2,1:T(8,128)} fusion(f32[16,128,16,128]{3,1,2,0:T(8,128)} %bitcast.162), kind=kOutput, calls=%fused_computation.57 | convolution fusion | flops 6442680320 | bytes 33554432 | tf_op jit(solution)/shard_map/fzyx,zk->fkyx/dot_general | solution.py:21
  1061.5 22.3 %fusion.56 = f32[128,16,16,128]{3,0,2,1:T(8,128)} fusion(f32[16,128,16,128]{3,1,2,0:T(8,128)} %bitcast.156), kind=kOutput, calls=%fused_computation.69 | convolution fusion | flops 6442680320 | bytes 33554432 | tf_op jit(solution)/shard_map/fzyx,zk->fkyx/dot_general | solution.py:21
  1083.9 26.3 %add_multiply_fusion = f32[128,16,16,128]{3,0,2,1:T(8,128)} fusion(f32[128,16,16,128]{3,0,2,1:T(8,128)} %fusion.44, f32[16,128,16,128]{3,1,2,0:T(8,128)} %bitcast.157, f32[128,16,128]{2,0,1:T(8,128)S(1)} %add_divide_fusion), kind=kOutput, calls=%fused_computation.20 | convolution fusion | flops 6455263232 | bytes 51380224 | tf_op jit(solution)/shard_map/fzyx,zk->fkyx/dot_general | solution.py:21
  1110.2 26.6 %subtract_multiply_fusion = f32[128,16,16,128]{3,0,2,1:T(8,128)} fusion(f32[128,16,16,128]{3,0,2,1:T(8,128)} %fusion.56, f32[16,128,16,128]{3,1,2,0:T(8,128)} %bitcast.163, f32[128,16,128]{2,0,1:T(8,128)S(1)} %add_divide_fusion), kind=kOutput, calls=%fused_computation.21 | convolution fusion | flops 6455263232 | bytes 51380224 | tf_op jit(solution)/shard_map/fzyx,zk->fkyx/dot_general | solution.py:21
  1136.8 22.3 %fusion.10 = f32[128,16,16,128]{3,0,2,1:T(8,128)} fusion(f32[128,16,16,128]{3,0,2,1:T(8,128)} %add_multiply_fusion), kind=kOutput, calls=%fused_computation.10 | convolution fusion | flops 6442680320 | bytes 33554432 | tf_op jit(solution)/shard_map/fzyx,zk->fkyx/dot_general | solution.py:21
  1159.1 24.8 %subtract_bitcast_fusion = f32[16,128,16,128]{3,1,2,0:T(8,128)} fusion(f32[128,16,16,128]{3,0,2,1:T(8,128)} %fusion.10, f32[128,16,16,128]{3,0,2,1:T(8,128)} %subtract_multiply_fusion), kind=kOutput, calls=%fused_computation.19 | convolution fusion | flops 6446874624 | bytes 50331648 | tf_op jit(solution)/shard_map/fzyx,zk->fkyx/dot_general | solution.py:21
  1183.8 17.8 copy.38
  1201.6 6.1 all-to-all-start.2
  1207.7 22.3 %fusion.8 = f32[128,16,16,128]{3,0,2,1:T(8,128)} fusion(f32[128,16,16,128]{3,0,2,1:T(8,128)} %add_multiply_fusion), kind=kOutput, calls=%fused_computation.8 | convolution fusion | flops 6442680320 | bytes 33554432 | tf_op jit(solution)/shard_map/fzyx,zk->fkyx/dot_general | solution.py:21
  1230.0 24.8 %add_bitcast_fusion = f32[16,128,16,128]{3,1,2,0:T(8,128)} fusion(f32[128,16,16,128]{3,0,2,1:T(8,128)} %fusion.8, f32[128,16,16,128]{3,0,2,1:T(8,128)} %subtract_multiply_fusion), kind=kOutput, calls=%fused_computation.18 | convolution fusion | flops 6446874624 | bytes 50331648 | tf_op jit(solution)/shard_map/fzyx,zk->fkyx/dot_general | solution.py:21
  1254.8 17.7 copy.43
  1272.5 297.0 %all-to-all-done.2 = f32[16,128,16,128]{3,2,0,1:T(8,128)} async-done(((f32[16,128,16,128]{3,2,0,1:T(8,128)}), f32[16,128,16,128]{3,2,0,1:T(8,128)}, u32[]{:S(2)}, u32[]{:S(2)}) %all-to-all-start.2) | async-done | bytes 16777248 | tf_op jit(solution)/shard_map/all_to_all | solution.py:80
  1569.6 6.0 all-to-all-start.3
  1575.5 11.9 copy.39
  1587.5 349.1 %all-to-all-done.3 = f32[16,128,16,128]{3,2,0,1:T(8,128)} async-done(((f32[16,128,16,128]{3,2,0,1:T(8,128)}), f32[16,128,16,128]{3,2,0,1:T(8,128)}, u32[]{:S(2)}, u32[]{:S(2)}) %all-to-all-start.3) | async-done | bytes 16777248 | tf_op jit(solution)/shard_map/all_to_all | solution.py:81
  1936.6 11.9 copy.44
  1948.5 22.2 %fusion.41 = f32[128,16,16,128]{3,0,2,1:T(8,128)} fusion(f32[16,16,128,128]{3,2,1,0:T(8,128)} %bitcast.160), kind=kOutput, calls=%fused_computation.54 | convolution fusion | flops 6442680320 | bytes 33554432 | tf_op jit(solution)/shard_map/fzyx,yk->fzkx/dot_general | solution.py:21
  1970.8 22.5 %fusion.59 = f32[128,16,16,128]{3,0,2,1:T(8,128)} fusion(f32[16,16,128,128]{3,2,1,0:T(8,128)} %bitcast.158), kind=kOutput, calls=%fused_computation.72 | convolution fusion | flops 6442680320 | bytes 33554432 | tf_op jit(solution)/shard_map/fzyx,yk->fzkx/dot_general | solution.py:21
  1993.3 24.8 %convolution_add_fusion = f32[128,16,16,128]{3,0,2,1:T(8,128)} fusion(f32[128,16,16,128]{3,0,2,1:T(8,128)} %fusion.41, f32[16,16,128,128]{3,2,1,0:T(8,128)} %bitcast.159), kind=kOutput, calls=%fused_computation.28 | convolution fusion | flops 6446874624 | bytes 50331648 | tf_op jit(solution)/shard_map/fzyx,yk->fzkx/dot_general | solution.py:21
  2018.1 0.0 copy-start
  2018.1 19.8 fusion
  2037.9 0.0 copy-done
  2037.9 16.8 fusion.2
  2054.7 24.8 %convolution_subtract_fusion = f32[128,16,16,128]{3,0,2,1:T(8,128)} fusion(f32[128,16,16,128]{3,0,2,1:T(8,128)} %fusion.59, f32[16,16,128,128]{3,2,1,0:T(8,128)} %bitcast.161), kind=kOutput, calls=%fused_computation.29 | convolution fusion | flops 6446874624 | bytes 50331648 | tf_op jit(solution)/shard_map/fzyx,yk->fzkx/dot_general | solution.py:21
  2079.5 0.0 copy-start.1
  2079.5 20.3 multiply_reduce_fusion
  2099.8 0.0 copy-done.1
  2099.8 17.9 multiply_reduce_fusion.1
  2117.7 1.6 add_negate_fusion
  (2 shorter events, 0.0 us)
Async XLA Ops:
  6.5 111.0 %all-gather.2.cloned.1.call-start = ((), (), s32[]{:S(2)}) async-start(), calls=%async_computation.4 | async-start | bytes 20971520 | tf_op jit(solution)/shard_map/all_gather | solution.py:51
  8.7 124.7 %copy-start.2 = (f32[2,16,128,128]{3,2,1,0:T(8,128)S(1)}, f32[2,16,128,128]{3,2,1,0:T(8,128)}, u32[]{:S(2)}) copy-start(f32[2,16,128,128]{3,2,1,0:T(8,128)} %param.3) | copy-start | bytes 6291460
  289.4 369.5 %all-to-all-start = ((f32[16,16,128,128]{3,1,0,2:T(8,128)}), f32[16,16,128,128]{3,1,0,2:T(8,128)}, u32[]{:S(2)}, u32[]{:S(2)}) async-start(f32[16,16,128,128]{3,1,0,2:T(8,128)} %copy.26), calls=%async_computation | async-start | bytes 33554432 | tf_op jit(solution)/shard_map/all_to_all | solution.py:71
  658.9 368.6 %all-to-all-start.1 = ((f32[16,16,128,128]{3,1,0,2:T(8,128)}), f32[16,16,128,128]{3,1,0,2:T(8,128)}, u32[]{:S(2)}, u32[]{:S(2)}) async-start(f32[16,16,128,128]{3,1,0,2:T(8,128)} %copy.31), calls=%async_computation.1 | async-start | bytes 33554432 | tf_op jit(solution)/shard_map/all_to_all | solution.py:72
  1201.6 368.0 %all-to-all-start.2 = ((f32[16,128,16,128]{3,2,0,1:T(8,128)}), f32[16,128,16,128]{3,2,0,1:T(8,128)}, u32[]{:S(2)}, u32[]{:S(2)}) async-start(f32[16,128,16,128]{3,2,0,1:T(8,128)} %copy.38), calls=%async_computation.2 | async-start | bytes 33554432 | tf_op jit(solution)/shard_map/all_to_all | solution.py:80
  1569.6 367.0 %all-to-all-start.3 = ((f32[16,128,16,128]{3,2,0,1:T(8,128)}), f32[16,128,16,128]{3,2,0,1:T(8,128)}, u32[]{:S(2)}, u32[]{:S(2)}) async-start(f32[16,128,16,128]{3,2,0,1:T(8,128)} %copy.43), calls=%async_computation.3 | async-start | bytes 33554432 | tf_op jit(solution)/shard_map/all_to_all | solution.py:81
  2018.1 19.8 copy-start
  2079.5 20.3 copy-start.1
Sparse Core Ops, SparseCore 0:
  8.9 108.6 all-gather.1
where the time goes:
time: 2140 us; the launch traced here: 2130 us
  waiting for transfers between devices  1400 us (65%)
  matrix products  534 us (25%)
  local copies, waits for them, and re-layouts  120 us (6%)
  other arithmetic  30.9 us (1%)
  starting transfers between devices  24 us (1%)
    dot_general x24, matrix products, apply(): jnp.einsum(form, values, table, precision=lax.Precision.HIGHEST, preferre...  534 us
    all_to_all x1, waiting for transfers between devices, per_device(): lax.all_to_all(imag_part, 'slab', split_axis=2, concat_axis=1, tiled=True)  350 us
    all_to_all x1, waiting for transfers between devices, per_device(): lax.all_to_all(col_imag, 'slab', split_axis=1, concat_axis=2, tiled=True)  349 us
    all_to_all x1, waiting for transfers between devices, per_device(): lax.all_to_all(real_part, 'slab', split_axis=2, concat_axis=1, tiled=True)  297 us
    all_to_all x1, waiting for transfers between devices, per_device(): lax.all_to_all(col_real, 'slab', split_axis=1, concat_axis=2, tiled=True)  297 us
    all_gather x1, waiting for transfers between devices, per_device(): source = lax.all_gather(blocks, 'band', axis=0, tiled=True)  109 us
  transfers between devices with their start and end apart: 5, of which 5 were waited for; matrix products, arithmetic and copies ran while one was open for 7% of the time, Pallas kernels for 0%

commit v1 on v0

--- a/solution.py
+++ b/solution.py
@@ -1,11 +1,15 @@
+import functools
 import math
 
 import jax
 import jax.numpy as jnp
 from jax import lax
+from jax.experimental import pallas as pl
+from jax.experimental.pallas import tpu as pltpu
 from jax.sharding import PartitionSpec as P
 
 KAPPA_SQ = 0.01
+F32, BF16 = (jnp.float32, jnp.bfloat16)
 
 
 def dft_tables(grid_len):
@@ -39,7 +43,7 @@
     return 4.0 * math.pi / (squared + KAPPA_SQ)
 
 
-def per_device(resident, blocks, occupation):
+def sliced_grids(resident, blocks, occupation):
     orb_count, plane_count, grid_len, _ = resident.shape
     local_src = blocks.shape[0]
     group_count = lax.axis_size("band")
@@ -93,6 +97,289 @@
     return -summed
 
 
+def halves(value):
+    top = value.astype(BF16)
+    return (top, (value - top.astype(F32)).astype(BF16))
+
+
+def cas_tables(grid_len):
+    indices = jnp.arange(grid_len, dtype=jnp.int32)
+    product = indices[:, None] * indices[None, :] % grid_len
+    angles = product.astype(F32) * (2.0 * math.pi / grid_len)
+    table = jnp.cos(angles) + jnp.sin(angles)
+    top = lax.reduce_precision(table, 8, 7)
+    high, low = (top.astype(BF16), (table - top).astype(BF16))
+    zero = jnp.zeros_like(high)
+    right = jnp.block([[high, low], [high, zero]])
+    left = jnp.block([[high, high], [low, zero]])
+    return (right, left)
+
+
+def times_table(rows, right):
+    grid_len = rows.shape[1]
+    both = jnp.dot(jnp.concatenate(halves(rows), 1), right, preferred_element_type=F32)
+    return both[:, :grid_len] + both[:, grid_len:]
+
+
+def table_times(left, cols):
+    grid_len = cols.shape[0]
+    both = jnp.dot(left, jnp.concatenate(halves(cols), 0), preferred_element_type=F32)
+    return both[:grid_len] + both[grid_len:]
+
+
+def beside(rows, count):
+    size = rows.shape[0] // count
+    return jnp.concatenate([rows[k * size : (k + 1) * size] for k in range(count)], 1)
+
+
+def below(cols, count):
+    size = cols.shape[1] // count
+    return jnp.concatenate([cols[:, k * size : (k + 1) * size] for k in range(count)], 0)
+
+
+STEP = 16
+
+
+def exchange_kernel(grid_len, slots, first, where_ref, occ_ref, gx_ref, gz_ref, right_ref, left_ref, *refs):
+    refs = list(refs)
+    res_refs = [refs.pop(0) for _ in range(2 * slots - 1)]
+    src_refs = [refs.pop(0) for _ in range(4)]
+    old_refs = [] if first else [refs.pop(0) for _ in range(slots)]
+    out_refs = [refs.pop(0) for _ in range(slots)]
+    res, src, work, acc, res_sem, src_sem, old_sem, out_sem = refs
+    n = grid_len
+    slot_len = n // slots
+    slab_len = slot_len // 2
+    slabs = 2 * slots
+    place = where_ref[8]
+
+    def res_copy(ref, slot):
+        return pltpu.make_async_copy(ref, res.at[pl.ds(slot * slot_len, slot_len)], res_sem.at[slot])
+
+    def src_copy(ref, slab):
+        return pltpu.make_async_copy(ref, src.at[pl.ds(slab * slab_len, slab_len)], src_sem.at[slab])
+
+    def old_copy(slot):
+        return pltpu.make_async_copy(old_refs[slot], acc.at[pl.ds(slot * slot_len, slot_len)], old_sem.at[slot])
+
+    def out_copy(slot):
+        return pltpu.make_async_copy(acc.at[pl.ds(slot * slot_len, slot_len)], out_refs[slot], out_sem.at[slot])
+
+    res_copy(res_refs[0], 0).start()
+    for k in range(4):
+        for half in range(2):
+            src_copy(src_refs[k].at[half], where_ref[2 * k + half]).start()
+    for slot in range(1, slots):
+        down, up = (res_refs[slot], res_refs[slots - 1 + slots - slot])
+
+        @pl.when(place + slot < slots)
+        def _(down=down, slot=slot):
+            res_copy(down, slot).start()
+
+        @pl.when(place + slot >= slots)
+        def _(up=up, slot=slot):
+            res_copy(up, slot).start()
+
+    for slot in range(slots):
+        if not first:
+            old_copy(slot).start()
+    right = right_ref[...]
+    left = left_ref[...]
+
+    def forward(i, carry):
+        z = i * STEP
+        value = (res[pl.ds(z, STEP)] * src[pl.ds(z, STEP)]).reshape(STEP * n, n)
+        value = table_times(left, beside(times_table(value, right), STEP))
+        for k in range(STEP):
+            work[pl.ds((z + k) * n, n), :] = value[:, k * n : (k + 1) * n]
+        return carry
+
+    for slab in range(slabs):
+        if slab % 2 == 0:
+            res_copy(res_refs[0], slab // 2).wait()
+        src_copy(src_refs[0].at[0], slab).wait()
+        lax.fori_loop(slab * slab_len // STEP, (slab + 1) * slab_len // STEP, forward, 0)
+
+    scale = 4.0 * math.pi / float(n) ** 3
+
+    def columns(i, carry):
+        y = i * STEP
+        value = jnp.concatenate([work[pl.ds(y + k, n, stride=n), :] for k in range(STEP)], 1)
+        value = table_times(left, value)
+        plane = gz_ref[...] + gx_ref[...] + KAPPA_SQ
+        value = jnp.concatenate(
+            [
+                value[:, k * n : (k + 1) * n] * (scale / (plane + gz_ref[pl.ds(y + k, 1), :]))
+                for k in range(STEP)
+            ],
+            1,
+        )
+        value = table_times(left, value)
+        for k in range(STEP):
+            work[pl.ds(y + k, n, stride=n), :] = value[:, k * n : (k + 1) * n]
+        return carry
+
+    lax.fori_loop(0, n // STEP, columns, 0)
+    weight = -occ_ref[0]
+
+    def backward(i, carry):
+        z = i * STEP
+        value = jnp.concatenate([work[pl.ds((z + k) * n, n), :] for k in range(STEP)], 1)
+        value = times_table(below(table_times(left, value), STEP), right).reshape(STEP, n, n)
+        value = value * (src[pl.ds(z, STEP)] * weight)
+        if not first:
+            value = value + acc[pl.ds(z, STEP)]
+        acc[pl.ds(z, STEP)] = value
+        return carry
+
+    order = list(range(1, slots)) + [0]
+    for slot in order:
+        if not first:
+            old_copy(slot).wait()
+        lax.fori_loop(slot * slot_len // STEP, (slot + 1) * slot_len // STEP, backward, 0)
+        out_copy(slot).start()
+    for slot in order:
+        out_copy(slot).wait()
+
+
+def exchange(where, occ, res_pieces, src_pieces, old, tables, waves):
+    right, left = tables
+    slots = (len(res_pieces) + 1) // 2
+    slot_len, n, _ = res_pieces[0].shape
+    any_spec = pl.BlockSpec(memory_space=pl.ANY)
+    vmem_spec = pl.BlockSpec(memory_space=pltpu.VMEM)
+    smem_spec = pl.BlockSpec(memory_space=pltpu.SMEM)
+    pieces = [*res_pieces, *src_pieces, *(old or [])]
+    grid = pltpu.VMEM((n, n, n), F32)
+    return pl.pallas_call(
+        functools.partial(exchange_kernel, n, slots, old is None),
+        out_shape=[jax.ShapeDtypeStruct((slot_len, n, n), F32)] * slots,
+        in_specs=[smem_spec] * 2 + [vmem_spec] * 4 + [any_spec] * len(pieces),
+        out_specs=[any_spec] * slots,
+        scratch_shapes=[
+            grid,
+            grid,
+            pltpu.VMEM((n * n, n), F32),
+            grid,
+            pltpu.SemaphoreType.DMA((slots,)),
+            pltpu.SemaphoreType.DMA((2 * slots,)),
+            pltpu.SemaphoreType.DMA((slots,)),
+            pltpu.SemaphoreType.DMA((slots,)),
+        ],
+        compiler_params=pltpu.CompilerParams(vmem_limit_bytes=60 * 1024 * 1024),
+        cost_estimate=pl.CostEstimate(flops=48 * n**4, bytes_accessed=16 * n**3, transcendentals=0),
+        name="exchange",
+    )(where, occ.reshape(1), waves[None, :], jnp.broadcast_to(waves[:, None], (n, n)), right, left, *pieces)
+
+
+def whole_grids(resident, blocks, occupation):
+    count_res, slab_len, n, _ = resident.shape
+    slabs = lax.axis_size("slab")
+    bands = lax.axis_size("band")
+    planes = slabs // 2
+    names = ("band", "slab")
+    coords = [
+        (x, c, z, y) for x in range(2) for c in range(2) for z in range(planes) for y in range(2)
+    ]
+
+    def flat(x, c, z, y):
+        return ((x * 2 + c) * planes + z) * 2 + y
+
+    def send(value, rule):
+        pairs = []
+        for coord in coords:
+            target = rule(*coord)
+            if target is not None:
+                pairs.append((flat(*coord), flat(*target)))
+        return lax.ppermute(value, names, pairs)
+
+    band, slab = (lax.axis_index("band"), lax.axis_index("slab"))
+    c, z, y = (band % 2, slab // 2, slab % 2)
+    x = band // 2
+
+    def swap_x(v):
+        return send(v, lambda x, c, z, y: (1 - x, c, z, y))
+
+    def swap_c(v):
+        return send(v, lambda x, c, z, y: (x, 1 - c, z, y))
+
+    def swap_y(v):
+        return send(v, lambda x, c, z, y: (x, c, z, 1 - y))
+
+    low = z < planes // 2
+    first_half, last_half = (blocks[:2], blocks[2:])
+
+    def to_low(x, c, z, y):
+        return (x, z, 2 * c + x, y) if z < 2 else (1 - x, z - 2, 2 * c + x, y)
+
+    def to_high(x, c, z, y):
+        return (x, z - 2, 2 * c + x, y) if z >= 2 else (1 - x, z, 2 * c + x, y)
+
+    part_1 = send(jnp.where(low, first_half, last_half), to_low)
+    part_2 = send(jnp.where(low, last_half, first_half), to_high)
+    own = [jnp.stack([part_1[k], part_2[k]]) for k in range(2)]
+
+    straight = send(lax.dynamic_index_in_dim(resident, y, 0, False), lambda x, c, z, y: (x, y, z, c))
+    crossed = send(lax.dynamic_index_in_dim(resident, 1 - y, 0, False), lambda x, c, z, y: (x, 1 - y, z, c))
+    quarter = jnp.where(
+        c == 0, jnp.concatenate([straight, crossed]), jnp.concatenate([crossed, straight])
+    )
+    downs, ups = ([], [])
+    down = up = quarter
+    for step in range(1, planes):
+        down = send(down, lambda x, c, z, y: (x, c, z - 1, y) if 1 <= z <= planes - step else None)
+        up = send(up, lambda x, c, z, y: (x, c, z + 1, y) if step - 1 <= z < planes - 1 else None)
+        downs.append(down)
+        ups.append(up)
+    res_pieces = [quarter, *downs, *ups]
+
+    beside_y = [swap_y(own[0]), swap_y(own[1])]
+    beside_x = [swap_x(own[0]), swap_x(own[1])]
+    corner = [swap_y(beside_x[0]), swap_x(beside_y[1])]
+    pieces = [(own[0], beside_y[0]), (own[1], beside_y[1]), (beside_x[0], corner[0]), (beside_x[1], corner[1])]
+
+    turned = (x + z) % 2
+    quad = 2 * (z % 2) + z // 2
+    tables = cas_tables(n)
+    waves = wave_of(jnp.arange(n, dtype=jnp.int32), n) ** 2
+    total = None
+    for index, (same, other) in enumerate(pieces):
+        flip = turned if index < 2 else 1 - turned
+        where = []
+        for core in (c, 1 - c):
+            for parity in (y, 1 - y):
+                for half in (flip, 1 - flip):
+                    where.append((core + 2 * half + planes - z) % planes * 2 + parity)
+        where = jnp.stack([*where, z]).astype(jnp.int32)
+        occ = lax.dynamic_index_in_dim(occupation, 4 * quad + 2 * flip + index % 2, 0, False)
+        total = exchange(where, occ, res_pieces, [same, other, swap_c(same), swap_c(other)], total, tables, waves)
+
+    down = up = None
+    for step in range(1, planes):
+        low_part, high_part = (total[step], total[planes - step])
+        if step > 1:
+            low_part, high_part = (low_part + down, high_part + up)
+        down = send(low_part, lambda x, c, z, y: (x, c, z - 1, y) if z >= planes - step and z >= 1 else None)
+        up = send(high_part, lambda x, c, z, y: (x, c, z + 1, y) if z <= step - 1 and z < planes - 1 else None)
+    summed = total[0] + down + up
+    near, far = (summed[:slab_len], summed[slab_len:])
+    back = send(jnp.where(c == 0, near, far), lambda x, c, z, y: (x, y, z, c))
+    cross = send(jnp.where(c == 0, far, near), lambda x, c, z, y: (x, y, z, 1 - c))
+    return jnp.where(y == 0, jnp.stack([back, cross]), jnp.stack([cross, back]))
+
+
+def per_device(resident, blocks, occupation):
+    if (
+        lax.axis_size("band") == 4
+        and lax.axis_size("slab") == 8
+        and resident.shape[0] == 2
+        and blocks.shape[0] == 4
+        and resident.shape[1] % STEP == 0
+    ):
+        return whole_grids(resident, blocks, occupation)
+    return sliced_grids(resident, blocks, occupation)
+
+
 def solution(mesh):
     placed = (P("band", "slab", None, None), P("band", "slab", None, None), P())
     return jax.shard_map(

time: 2140 us -> 658 us (0.31)
  waiting for transfers between devices: 1400 us -> 352 us
  matrix products: 534 us -> 0 us
  Pallas kernels: 0 us -> 137 us
  local copies, waits for them, and re-layouts: 120 us -> 8.54 us
  starting transfers between devices: 24 us -> 133 us
    all_to_all x4 -> x0, waiting for transfers between devices: 1290 us -> none  [the longest x1 350 us: per_device(): lax.all_to_all(imag_part, 'slab', split_axis=2, concat_axis=1, tiled=True)]
    dot_general x24 -> x0, matrix products: 534 us -> none  [apply(): jnp.einsum(form, values, table, precision=lax.Precision.HIGHEST, preferre...]
    ppermute x0 -> x32, waiting for transfers between devices: none -> 352 us  [send(): return lax.ppermute(value, names, pairs)]
    pallas_call x0 -> x4, Pallas kernels: none -> 137 us  [exchange(): pl.pallas_call(functools.partial(exchange_kernel, n, slots, old is None),...]
    ppermute x0 -> x32, starting transfers between devices: none -> 133 us  [send(): return lax.ppermute(value, names, pairs)]
    all_gather x1 -> x0, waiting for transfers between devices: 109 us -> none  [per_device(): source = lax.all_gather(blocks, 'band', axis=0, tiled=True)]
    all_to_all x4 -> x0, local copies, waits for them, and re-layouts: 47.7 us -> none  [the longest x1 11.9 us: per_device(): lax.all_to_all(imag_part, 'slab', split_axis=2, concat_axis=1, tiled=True)]
    sub x2 -> x0, local copies, waits for them, and re-layouts: 35.5 us -> none  [transform(): return (real_cos - sign_val * imag_sin, imag_cos + sign_val * real_sin)]
  transfers between devices with their start and end apart: 5 -> 32, of which waited for: 5 -> 13; matrix products, arithmetic and copies ran while one was open for 7% -> 2% of each run, Pallas kernels for 0% -> 16%
where the time goes in v1:
time: 658 us; the launch traced here: 646 us
  waiting for transfers between devices  352 us (53%)
  Pallas kernels  137 us (21%)
  starting transfers between devices  133 us (20%)
  other arithmetic  15.5 us (2%)
  local copies, waits for them, and re-layouts  8.54 us (1%)
    ppermute x32, waiting for transfers between devices, send(): return lax.ppermute(value, names, pairs)  352 us
    pallas_call x4, Pallas kernels, exchange(): pl.pallas_call(functools.partial(exchange_kernel, n, slots, old is None),...  137 us
    ppermute x32, starting transfers between devices, send(): return lax.ppermute(value, names, pairs)  133 us
  transfers between devices with their start and end apart: 32, of which 13 were waited for; matrix products, arithmetic and copies ran while one was open for 2% of the time, Pallas kernels for 16%

profile of v1, /device:TPU:0, one launch (start us, length us, event | category | flops | bytes accessed | tf_op | source)
XLA Modules:
  0.0 646.5 jit_solution(9233986885629319650)
XLA Ops:
  0.0 5.0 slice_select_fusion.1
  5.0 17.2 %collective-permute-start.8 = (f32[2,16,128,128]{3,2,1,0:T(8,128)}, f32[2,16,128,128]{3,2,1,0:T(8,128)}, u32[]{:S(2)}, u32[]{:S(2)}) collective-permute-start(f32[2,16,128,128]{3,2,1,0:T(8,128)} %get-tuple-element.37), channel_id=1, source_target_pairs={{0,0},{1,1},{2,8},{3,9},{4,16},{5,17},{6,24},{7,25},{8,4},{9,5},{1... | collective-permute-start | bytes 6291464 | tf_op jit(solution)/shard_map/ppermute | solution.py:294
  22.2 1.9 collective-permute-start.9
  24.1 1.2 dynamic-slice_bitcast_fusion.1
  25.3 1.9 collective-permute-start
  27.2 3.2 collective-permute-start.1
  30.3 24.1 %collective-permute-done.1 = f32[16,128,128]{2,1,0:T(8,128)S(1)} collective-permute-done((f32[16,128,128]{2,1,0:T(8,128)S(1)}, f32[16,128,128]{2,1,0:T(8,128)S(1)}, u32[]{:S(2)}, u32[]{:S(2)}) %collective-permute-start.1) | collective-permute-done | bytes 1048608 | tf_op jit(solution)/shard_map/ppermute | solution.py:294
  54.4 0.3 maximum_select_fusion.refs_0_
  54.7 1.3 collective-permute-start.2
  56.0 4.7 collective-permute-start.5
  60.7 1.7 fusion.18
  62.4 62.8 %collective-permute-done.9 = f32[2,16,128,128]{3,2,1,0:T(8,128)} collective-permute-done((f32[2,16,128,128]{3,2,1,0:T(8,128)}, f32[2,16,128,128]{3,2,1,0:T(8,128)}, u32[]{:S(2)}, u32[]{:S(2)}) %collective-permute-start.9) | collective-permute-done | bytes 2097184 | tf_op jit(solution)/shard_map/ppermute | solution.py:294
  125.2 1.7 fusion.19
  126.9 0.2 pad_maximum_fusion.1.refs_7_
  127.1 1.2 collective-permute-start.21
  128.4 20.8 %collective-permute-start.22 = (f32[2,16,128,128]{3,2,1,0:T(8,128)S(1)}, f32[2,16,128,128]{3,2,1,0:T(8,128)S(1)}, u32[]{:S(2)}, u32[]{:S(2)}) collective-permute-start(f32[2,16,128,128]{3,2,1,0:T(8,128)S(1)} %pad_maximum_fusion.1.refs_7_), channel_id=1, source_target_pairs={{0,8},{1,9},{2,10},{3,11},{4,12},{5,13},{6,14},{7,15},{8,0},{9,1},... | collective-permute-start | bytes 6291464 | tf_op jit(solution)/shard_map/ppermute | solution.py:294
  149.2 1.5 pad_maximum_fusion.refs_7_
  150.6 0.5 collective-permute-start.11
  151.2 51.9 %collective-permute-done.2.refs_1_ = f32[32,128,128]{2,1,0:T(8,128)S(1)} collective-permute-done((f32[32,128,128]{2,1,0:T(8,128)S(1)}, f32[32,128,128]{2,1,0:T(8,128)S(1)}, u32[]{:S(2)}, u32[]{:S(2)}) %collective-permute-start.2) | collective-permute-done | bytes 2097184 | tf_op jit(solution)/shard_map/ppermute | solution.py:294
  203.1 1.3 collective-permute-start.3
  204.4 2.0 collective-permute-start.6
  206.5 14.4 %collective-permute-start.23 = (f32[2,16,128,128]{3,2,1,0:T(8,128)S(1)}, f32[2,16,128,128]{3,2,1,0:T(8,128)S(1)}, u32[]{:S(2)}, u32[]{:S(2)}) collective-permute-start(f32[2,16,128,128]{3,2,1,0:T(8,128)S(1)} %collective-permute-done.21.refs_8_), channel_id=1, source_target_pairs={{0,8},{1,9},{2,10},{3,11},{4,12},{5,13},{6,14},{7,15},{8,0},{9,1},... | collective-permute-start | bytes 6291464 | tf_op jit(solution)/shard_map/ppermute | solution.py:294
  220.9 8.3 %collective-permute-done.15.refs_7_ = f32[2,16,128,128]{3,2,1,0:T(8,128)} collective-permute-done((f32[2,16,128,128]{3,2,1,0:T(8,128)S(1)}, f32[2,16,128,128]{3,2,1,0:T(8,128)}, u32[]{:S(2)}, u32[]{:S(2)}) %collective-permute-start.15) | collective-permute-done | bytes 2097184 | tf_op jit(solution)/shard_map/ppermute | solution.py:294
  229.2 1.7 collective-permute-start.16
  231.0 5.5 collective-permute-done.3.refs_2_
  236.5 1.3 collective-permute-start.4
  237.8 2.1 collective-permute-start.7
  239.9 7.3 %collective-permute-start.10 = (f32[2,16,128,128]{3,2,1,0:T(8,128)}, f32[2,16,128,128]{3,2,1,0:T(8,128)}, u32[]{:S(2)}, u32[]{:S(2)}) collective-permute-start(f32[2,16,128,128]{3,2,1,0:T(8,128)} %pad_maximum_fusion.refs_7_), channel_id=1, source_target_pairs={{0,16},{1,17},{2,18},{3,19},{4,20},{5,21},{6,22},{7,23},{8,24},{9,... | collective-permute-start | bytes 6291464 | tf_op jit(solution)/shard_map/ppermute | solution.py:294
  247.3 21.4 %collective-permute-done.16.refs_8_ = f32[2,16,128,128]{3,2,1,0:T(8,128)} collective-permute-done((f32[2,16,128,128]{3,2,1,0:T(8,128)}, f32[2,16,128,128]{3,2,1,0:T(8,128)}, u32[]{:S(2)}, u32[]{:S(2)}) %collective-permute-start.16) | collective-permute-done | bytes 2097184 | tf_op jit(solution)/shard_map/ppermute | solution.py:294
  268.7 0.7 stack.46.where_ref
  269.4 0.6 stack.43.where_ref
  270.0 0.7 fusion.20
  270.7 0.5 fusion.13.gx_ref
  271.2 0.3 reduce-precision_convert_fusion
  271.5 0.7 fusion.3
  272.2 18.6 %collective-permute-done.4.refs_3_ = f32[32,128,128]{2,1,0:T(8,128)} collective-permute-done((f32[32,128,128]{2,1,0:T(8,128)}, f32[32,128,128]{2,1,0:T(8,128)}, u32[]{:S(2)}, u32[]{:S(2)}) %collective-permute-start.4) | collective-permute-done | bytes 2097184 | tf_op jit(solution)/shard_map/ppermute | solution.py:294
  290.8 0.5 collective-permute-start.18
  291.4 0.7 broadcast_in_dim.8.gz_ref
  292.1 32.7 %exchange.4 = (f32[32,128,128]{2,1,0:T(8,128)}, f32[32,128,128]{2,1,0:T(8,128)}, f32[32,128,128]{2,1,0:T(8,128)}, f32[32,128,128]{2,1,0:T(8,128)}) custom-call(s32[9]{0:T(128)} %stack.46.where_ref, f32[1]{0:T(128)} %get-tuple-element.51.occ_ref, f32[1,128]{1,0:T(1,128)} %fusion.13.gx_ref, f32[128,128]{1,0:T(8,128)} %broadcast_in_dim.8.gz_ref, ...), custom_call_target="tpu_custom_call" | custom-call | flops 12884901888 | bytes 33554432 | tf_op jit(solution)/shard_map/exchange/pallas_call | solution.py:254
  324.8 1.9 collective-permute-start.13
  326.6 11.4 %collective-permute-done.12.refs_8_ = f32[2,16,128,128]{3,2,1,0:T(8,128)} collective-permute-done((f32[2,16,128,128]{3,2,1,0:T(8,128)}, f32[2,16,128,128]{3,2,1,0:T(8,128)}, u32[]{:S(2)}, u32[]{:S(2)}) %collective-permute-start.12) | collective-permute-done | bytes 2097184 | tf_op jit(solution)/shard_map/ppermute | solution.py:294
  338.0 33.7 %exchange.5 = (f32[32,128,128]{2,1,0:T(8,128)}, f32[32,128,128]{2,1,0:T(8,128)}, f32[32,128,128]{2,1,0:T(8,128)}, f32[32,128,128]{2,1,0:T(8,128)}) custom-call(s32[9]{0:T(128)} %stack.46.where_ref, f32[1]{0:T(128)} %get-tuple-element.54.occ_ref, f32[1,128]{1,0:T(1,128)} %fusion.13.gx_ref, f32[128,128]{1,0:T(8,128)} %broadcast_in_dim.8.gz_ref, ...), custom_call_target="tpu_custom_call" | custom-call | flops 12884901888 | bytes 33554432 | tf_op jit(solution)/shard_map/exchange/pallas_call | solution.py:254
  371.8 35.6 %exchange.6 = (f32[32,128,128]{2,1,0:T(8,128)}, f32[32,128,128]{2,1,0:T(8,128)}, f32[32,128,128]{2,1,0:T(8,128)}, f32[32,128,128]{2,1,0:T(8,128)}) custom-call(s32[9]{0:T(128)} %stack.43.where_ref, f32[1]{0:T(128)} %get-tuple-element.52.occ_ref, f32[1,128]{1,0:T(1,128)} %fusion.13.gx_ref, f32[128,128]{1,0:T(8,128)} %broadcast_in_dim.8.gz_ref, ...), custom_call_target="tpu_custom_call" | custom-call | flops 12884901888 | bytes 33554432 | tf_op jit(solution)/shard_map/exchange/pallas_call | solution.py:254
  407.4 1.3 copy-done.13
  408.7 35.1 %exchange.7 = (f32[32,128,128]{2,1,0:T(8,128)}, f32[32,128,128]{2,1,0:T(8,128)}, f32[32,128,128]{2,1,0:T(8,128)}, f32[32,128,128]{2,1,0:T(8,128)}) custom-call(s32[9]{0:T(128)} %stack.43.where_ref, f32[1]{0:T(128)} %get-tuple-element.53.occ_ref, f32[1,128]{1,0:T(1,128)} %fusion.13.gx_ref, f32[128,128]{1,0:T(8,128)} %broadcast_in_dim.8.gz_ref, ...), custom_call_target="tpu_custom_call" | custom-call | flops 12884901888 | bytes 33554432 | tf_op jit(solution)/shard_map/exchange/pallas_call | solution.py:254
  443.8 0.8 collective-permute-start.24
  444.6 11.7 %collective-permute-start.27 = (f32[32,128,128]{2,1,0:T(8,128)}, f32[32,128,128]{2,1,0:T(8,128)S(1)}, u32[]{:S(2)}, u32[]{:S(2)}) collective-permute-start(f32[32,128,128]{2,1,0:T(8,128)} %get-tuple-element.34), channel_id=1, source_target_pairs={{0,2},{1,3},{8,10},{9,11},{16,18},{17,19},{24,26},{25,27}} | collective-permute-start | bytes 6291464 | tf_op jit(solution)/shard_map/ppermute | solution.py:294
  456.3 41.3 %collective-permute-done.27 = f32[32,128,128]{2,1,0:T(8,128)S(1)} collective-permute-done((f32[32,128,128]{2,1,0:T(8,128)}, f32[32,128,128]{2,1,0:T(8,128)S(1)}, u32[]{:S(2)}, u32[]{:S(2)}) %collective-permute-start.27) | collective-permute-done | bytes 2097184 | tf_op jit(solution)/shard_map/ppermute | solution.py:294
  497.6 2.4 fusion.17
  500.1 0.8 collective-permute-start.25
  500.9 5.0 collective-permute-start.28
  506.0 0.3 add.331
  506.3 1.4 collective-permute-start.26
  507.7 38.3 %collective-permute-done.28 = f32[32,128,128]{2,1,0:T(8,128)S(1)} collective-permute-done((f32[32,128,128]{2,1,0:T(8,128)S(1)}, f32[32,128,128]{2,1,0:T(8,128)S(1)}, u32[]{:S(2)}, u32[]{:S(2)}) %collective-permute-start.28) | collective-permute-done | bytes 2097184 | tf_op jit(solution)/shard_map/ppermute | solution.py:294
  546.0 0.3 add.334
  546.3 20.3 %collective-permute-start.29 = (f32[32,128,128]{2,1,0:T(8,128)S(1)}, f32[32,128,128]{2,1,0:T(8,128)S(1)}, u32[]{:S(2)}, u32[]{:S(2)}) collective-permute-start(f32[32,128,128]{2,1,0:T(8,128)S(1)} %add.334), channel_id=1, source_target_pairs={{0,2},{1,3},{2,4},{3,5},{4,6},{5,7},{8,10},{9,11},{10,12},{11,13},... | collective-permute-start | bytes 6291464 | tf_op jit(solution)/shard_map/ppermute | solution.py:294
  566.7 43.4 %collective-permute-done.26 = f32[32,128,128]{2,1,0:T(8,128)S(1)} collective-permute-done((f32[32,128,128]{2,1,0:T(8,128)S(1)}, f32[32,128,128]{2,1,0:T(8,128)S(1)}, u32[]{:S(2)}, u32[]{:S(2)}) %collective-permute-start.26) | collective-permute-done | bytes 2097184 | tf_op jit(solution)/shard_map/ppermute | solution.py:294
  610.1 2.0 collective-permute-done.29
  612.1 0.6 add_add_fusion
  612.7 0.2 slice_select_fusion.3
  613.0 0.7 collective-permute-start.30
  613.7 6.5 %collective-permute-start.31 = (f32[16,128,128]{2,1,0:T(8,128)S(1)}, f32[16,128,128]{2,1,0:T(8,128)}, u32[]{:S(2)}, u32[]{:S(2)}) collective-permute-start(f32[16,128,128]{2,1,0:T(8,128)S(1)} %get-tuple-element.40), channel_id=1, source_target_pairs={{0,1},{1,9},{2,3},{3,11},{4,5},{5,13},{6,7},{7,15},{8,0},{9,8},{10... | collective-permute-start | bytes 3145736 | tf_op jit(solution)/shard_map/ppermute | solution.py:294
  620.2 22.9 %collective-permute-done.31 = f32[16,128,128]{2,1,0:T(8,128)} collective-permute-done((f32[16,128,128]{2,1,0:T(8,128)S(1)}, f32[16,128,128]{2,1,0:T(8,128)}, u32[]{:S(2)}, u32[]{:S(2)}) %collective-permute-start.31) | collective-permute-done | bytes 1048608 | tf_op jit(solution)/shard_map/ppermute | solution.py:294
  643.1 3.1 maximum_select_fusion.1
  (53 shorter events, 0.2 us)
Async XLA Ops:
  0.0 24.1 %copy-start.2 = (f32[2,16,128,128]{3,2,1,0:T(8,128)S(1)}, f32[2,16,128,128]{3,2,1,0:T(8,128)}, u32[]{:S(2)}) copy-start(f32[2,16,128,128]{3,2,1,0:T(8,128)} %param.3) | copy-start | bytes 6291460
  5.0 55.7 %collective-permute-start.8 = (f32[2,16,128,128]{3,2,1,0:T(8,128)}, f32[2,16,128,128]{3,2,1,0:T(8,128)}, u32[]{:S(2)}, u32[]{:S(2)}) collective-permute-start(f32[2,16,128,128]{3,2,1,0:T(8,128)} %get-tuple-element.37), channel_id=1, source_target_pairs={{0,0},{1,1},{2,8},{3,9},{4,16},{5,17},{6,24},{7,25},{8,4},{9,5},{1... | collective-permute-start | bytes 6291464 | tf_op jit(solution)/shard_map/ppermute | solution.py:294
  22.2 103.0 %collective-permute-start.9 = (f32[2,16,128,128]{3,2,1,0:T(8,128)}, f32[2,16,128,128]{3,2,1,0:T(8,128)}, u32[]{:S(2)}, u32[]{:S(2)}) collective-permute-start(f32[2,16,128,128]{3,2,1,0:T(8,128)} %get-tuple-element.38), channel_id=1, source_target_pairs={{0,16},{1,17},{2,24},{3,25},{4,0},{5,1},{6,8},{7,9},{8,20},{9,21},... | collective-permute-start | bytes 6291464 | tf_op jit(solution)/shard_map/ppermute | solution.py:294
  25.3 5.0 collective-permute-start
  27.2 27.2 %collective-permute-start.1 = (f32[16,128,128]{2,1,0:T(8,128)S(1)}, f32[16,128,128]{2,1,0:T(8,128)S(1)}, u32[]{:S(2)}, u32[]{:S(2)}) collective-permute-start(f32[16,128,128]{2,1,0:T(8,128)S(1)} %get-tuple-element.48), channel_id=1, source_target_pairs={{0,8},{1,0},{2,10},{3,2},{4,12},{5,4},{6,14},{7,6},{8,9},{9,1},{10... | collective-permute-start | bytes 3145736 | tf_op jit(solution)/shard_map/ppermute | solution.py:294
  54.7 72.2 %copy-start.3 = (f32[32,128,128]{2,1,0:T(8,128)}, f32[32,128,128]{2,1,0:T(8,128)S(1)}, u32[]{:S(2)}) copy-start(f32[32,128,128]{2,1,0:T(8,128)S(1)} %maximum_select_fusion.refs_0_) | copy-start | bytes 6291460
  54.7 148.4 %collective-permute-start.2 = (f32[32,128,128]{2,1,0:T(8,128)S(1)}, f32[32,128,128]{2,1,0:T(8,128)S(1)}, u32[]{:S(2)}, u32[]{:S(2)}) collective-permute-start(f32[32,128,128]{2,1,0:T(8,128)S(1)} %maximum_select_fusion.refs_0_), channel_id=1, source_target_pairs={{2,0},{3,1},{4,2},{5,3},{6,4},{7,5},{10,8},{11,9},{12,10},{13,11},... | collective-permute-start | bytes 6291464 | tf_op jit(solution)/shard_map/ppermute | solution.py:294
  56.0 147.1 %collective-permute-start.5 = (f32[32,128,128]{2,1,0:T(8,128)S(1)}, f32[32,128,128]{2,1,0:T(8,128)S(1)}, u32[]{:S(2)}, u32[]{:S(2)}) collective-permute-start(f32[32,128,128]{2,1,0:T(8,128)S(1)} %maximum_select_fusion.refs_0_), channel_id=1, source_target_pairs={{0,2},{1,3},{2,4},{3,5},{4,6},{5,7},{8,10},{9,11},{10,12},{11,13},... | collective-permute-start | bytes 6291464 | tf_op jit(solution)/shard_map/ppermute | solution.py:294
  127.1 76.0 %copy-start.4 = (f32[2,16,128,128]{3,2,1,0:T(8,128)}, f32[2,16,128,128]{3,2,1,0:T(8,128)S(1)}, u32[]{:S(2)}) copy-start(f32[2,16,128,128]{3,2,1,0:T(8,128)S(1)} %pad_maximum_fusion.1.refs_7_) | copy-start | bytes 6291460
  127.1 77.3 %collective-permute-start.21 = (f32[2,16,128,128]{3,2,1,0:T(8,128)S(1)}, f32[2,16,128,128]{3,2,1,0:T(8,128)S(1)}, u32[]{:S(2)}, u32[]{:S(2)}) collective-permute-start(f32[2,16,128,128]{3,2,1,0:T(8,128)S(1)} %pad_maximum_fusion.1.refs_7_), channel_id=1, source_target_pairs={{0,1},{1,0},{2,3},{3,2},{4,5},{5,4},{6,7},{7,6},{8,9},{9,8},{10,11... | collective-permute-start | bytes 6291464 | tf_op jit(solution)/shard_map/ppermute | solution.py:294
  128.4 78.1 %collective-permute-start.22 = (f32[2,16,128,128]{3,2,1,0:T(8,128)S(1)}, f32[2,16,128,128]{3,2,1,0:T(8,128)S(1)}, u32[]{:S(2)}, u32[]{:S(2)}) collective-permute-start(f32[2,16,128,128]{3,2,1,0:T(8,128)S(1)} %pad_maximum_fusion.1.refs_7_), channel_id=1, source_target_pairs={{0,8},{1,9},{2,10},{3,11},{4,12},{5,13},{6,14},{7,15},{8,0},{9,1},... | collective-permute-start | bytes 6291464 | tf_op jit(solution)/shard_map/ppermute | solution.py:294
  149.2 120.9 %copy-start.6 = (f32[16]{0:T(128)S(1)}, f32[16]{0:T(128)}, u32[]{:S(2)}) copy-start(f32[16]{0:T(128)} %param.5) | copy-start | bytes 196
  150.6 55.8 %collective-permute-start.11 = (f32[2,16,128,128]{3,2,1,0:T(8,128)}, f32[2,16,128,128]{3,2,1,0:T(8,128)}, u32[]{:S(2)}, u32[]{:S(2)}) collective-permute-start(f32[2,16,128,128]{3,2,1,0:T(8,128)} %pad_maximum_fusion.refs_7_), channel_id=1, source_target_pairs={{0,1},{1,0},{2,3},{3,2},{4,5},{5,4},{6,7},{7,6},{8,9},{9,8},{10,11... | collective-permute-start | bytes 6291464 | tf_op jit(solution)/shard_map/ppermute | solution.py:294
  203.1 89.0 %copy-start.7 = (f32[32,128,128]{2,1,0:T(8,128)}, f32[32,128,128]{2,1,0:T(8,128)S(1)}, u32[]{:S(2)}) copy-start(f32[32,128,128]{2,1,0:T(8,128)S(1)} %collective-permute-done.2.refs_1_) | copy-start | bytes 6291460
  203.1 26.1 %collective-permute-start.15 = (f32[2,16,128,128]{3,2,1,0:T(8,128)S(1)}, f32[2,16,128,128]{3,2,1,0:T(8,128)}, u32[]{:S(2)}, u32[]{:S(2)}) collective-permute-start(f32[2,16,128,128]{3,2,1,0:T(8,128)S(1)} %pad_maximum_fusion.1.refs_7_), channel_id=1, source_target_pairs={{0,16},{1,17},{2,18},{3,19},{4,20},{5,21},{6,22},{7,23},{8,24},{9,... | collective-permute-start | bytes 6291464 | tf_op jit(solution)/shard_map/ppermute | solution.py:294
  203.1 33.4 %copy-start.8 = (f32[32,128,128]{2,1,0:T(8,128)}, f32[32,128,128]{2,1,0:T(8,128)S(1)}, u32[]{:S(2)}) copy-start(f32[32,128,128]{2,1,0:T(8,128)S(1)} %collective-permute-done.5.refs_4_) | copy-start | bytes 6291460
  203.1 33.4 %collective-permute-start.3 = (f32[32,128,128]{2,1,0:T(8,128)S(1)}, f32[32,128,128]{2,1,0:T(8,128)}, u32[]{:S(2)}, u32[]{:S(2)}) collective-permute-start(f32[32,128,128]{2,1,0:T(8,128)S(1)} %collective-permute-done.2.refs_1_), channel_id=1, source_target_pairs={{2,0},{3,1},{4,2},{5,3},{10,8},{11,9},{12,10},{13,11},{18,16},{19,... | collective-permute-start | bytes 6291464 | tf_op jit(solution)/shard_map/ppermute | solution.py:294
  204.4 33.4 %copy-start.9 = (f32[2,16,128,128]{3,2,1,0:T(8,128)}, f32[2,16,128,128]{3,2,1,0:T(8,128)S(1)}, u32[]{:S(2)}) copy-start(f32[2,16,128,128]{3,2,1,0:T(8,128)S(1)} %collective-permute-done.21.refs_8_) | copy-start | bytes 6291460
  204.4 33.4 %collective-permute-start.6 = (f32[32,128,128]{2,1,0:T(8,128)S(1)}, f32[32,128,128]{2,1,0:T(8,128)}, u32[]{:S(2)}, u32[]{:S(2)}) collective-permute-start(f32[32,128,128]{2,1,0:T(8,128)S(1)} %collective-permute-done.5.refs_4_), channel_id=1, source_target_pairs={{2,4},{3,5},{4,6},{5,7},{10,12},{11,13},{12,14},{13,15},{18,20},{1... | collective-permute-start | bytes 6291464 | tf_op jit(solution)/shard_map/ppermute | solution.py:294
  206.5 40.8 %copy-start.10 = (f32[2,16,128,128]{3,2,1,0:T(8,128)}, f32[2,16,128,128]{3,2,1,0:T(8,128)S(1)}, u32[]{:S(2)}) copy-start(f32[2,16,128,128]{3,2,1,0:T(8,128)S(1)} %collective-permute-done.22.refs_9_) | copy-start | bytes 6291460
  206.5 33.4 %collective-permute-start.19 = (f32[2,16,128,128]{3,2,1,0:T(8,128)}, f32[2,16,128,128]{3,2,1,0:T(8,128)S(1)}, u32[]{:S(2)}, u32[]{:S(2)}) collective-permute-start(f32[2,16,128,128]{3,2,1,0:T(8,128)} %pad_maximum_fusion.refs_7_), channel_id=1, source_target_pairs={{0,8},{1,9},{2,10},{3,11},{4,12},{5,13},{6,14},{7,15},{8,0},{9,1},... | collective-permute-start | bytes 6291464 | tf_op jit(solution)/shard_map/ppermute | solution.py:294
  206.5 40.7 %collective-permute-start.23 = (f32[2,16,128,128]{3,2,1,0:T(8,128)S(1)}, f32[2,16,128,128]{3,2,1,0:T(8,128)S(1)}, u32[]{:S(2)}, u32[]{:S(2)}) collective-permute-start(f32[2,16,128,128]{3,2,1,0:T(8,128)S(1)} %collective-permute-done.21.refs_8_), channel_id=1, source_target_pairs={{0,8},{1,9},{2,10},{3,11},{4,12},{5,13},{6,14},{7,15},{8,0},{9,1},... | collective-permute-start | bytes 6291464 | tf_op jit(solution)/shard_map/ppermute | solution.py:294
  229.2 39.5 %collective-permute-start.16 = (f32[2,16,128,128]{3,2,1,0:T(8,128)}, f32[2,16,128,128]{3,2,1,0:T(8,128)}, u32[]{:S(2)}, u32[]{:S(2)}) collective-permute-start(f32[2,16,128,128]{3,2,1,0:T(8,128)} %collective-permute-done.15.refs_7_), channel_id=1, source_target_pairs={{0,1},{1,0},{2,3},{3,2},{4,5},{5,4},{6,7},{7,6},{8,9},{9,8},{10,11... | collective-permute-start | bytes 6291464 | tf_op jit(solution)/shard_map/ppermute | solution.py:294
  236.5 54.3 %collective-permute-start.4 = (f32[32,128,128]{2,1,0:T(8,128)}, f32[32,128,128]{2,1,0:T(8,128)}, u32[]{:S(2)}, u32[]{:S(2)}) collective-permute-start(f32[32,128,128]{2,1,0:T(8,128)} %collective-permute-done.3.refs_2_), channel_id=1, source_target_pairs={{2,0},{3,1},{10,8},{11,9},{18,16},{19,17},{26,24},{27,25}} | collective-permute-start | bytes 6291464 | tf_op jit(solution)/shard_map/ppermute | solution.py:294
  237.8 53.0 %collective-permute-start.7 = (f32[32,128,128]{2,1,0:T(8,128)}, f32[32,128,128]{2,1,0:T(8,128)}, u32[]{:S(2)}, u32[]{:S(2)}) collective-permute-start(f32[32,128,128]{2,1,0:T(8,128)} %collective-permute-done.6.refs_5_), channel_id=1, source_target_pairs={{4,6},{5,7},{12,14},{13,15},{20,22},{21,23},{28,30},{29,31}} | collective-permute-start | bytes 6291464 | tf_op jit(solution)/shard_map/ppermute | solution.py:294
  239.9 7.4 %copy-start.11 = (f32[2,16,128,128]{3,2,1,0:T(8,128)}, f32[2,16,128,128]{3,2,1,0:T(8,128)S(1)}, u32[]{:S(2)}) copy-start(f32[2,16,128,128]{3,2,1,0:T(8,128)S(1)} %collective-permute-done.19.refs_9_) | copy-start | bytes 6291460
  239.9 84.8 %collective-permute-start.10 = (f32[2,16,128,128]{3,2,1,0:T(8,128)}, f32[2,16,128,128]{3,2,1,0:T(8,128)}, u32[]{:S(2)}, u32[]{:S(2)}) collective-permute-start(f32[2,16,128,128]{3,2,1,0:T(8,128)} %pad_maximum_fusion.refs_7_), channel_id=1, source_target_pairs={{0,16},{1,17},{2,18},{3,19},{4,20},{5,21},{6,22},{7,23},{8,24},{9,... | collective-permute-start | bytes 6291464 | tf_op jit(solution)/shard_map/ppermute | solution.py:294
  247.2 21.5 %copy-start.12 = (f32[2,16,128,128]{3,2,1,0:T(8,128)}, f32[2,16,128,128]{3,2,1,0:T(8,128)S(1)}, u32[]{:S(2)}) copy-start(f32[2,16,128,128]{3,2,1,0:T(8,128)S(1)} %collective-permute-done.23.refs_10_) | copy-start | bytes 6291460
  247.2 90.8 %collective-permute-start.12 = (f32[2,16,128,128]{3,2,1,0:T(8,128)}, f32[2,16,128,128]{3,2,1,0:T(8,128)}, u32[]{:S(2)}, u32[]{:S(2)}) collective-permute-start(f32[2,16,128,128]{3,2,1,0:T(8,128)} %collective-permute-done.11.refs_8_), channel_id=1, source_target_pairs={{0,16},{1,17},{2,18},{3,19},{4,20},{5,21},{6,22},{7,23},{8,24},{9,... | collective-permute-start | bytes 6291464 | tf_op jit(solution)/shard_map/ppermute | solution.py:294
  268.7 69.3 %collective-permute-start.20 = (f32[2,16,128,128]{3,2,1,0:T(8,128)}, f32[2,16,128,128]{3,2,1,0:T(8,128)}, u32[]{:S(2)}, u32[]{:S(2)}) collective-permute-start(f32[2,16,128,128]{3,2,1,0:T(8,128)} %collective-permute-done.11.refs_8_), channel_id=1, source_target_pairs={{0,8},{1,9},{2,10},{3,11},{4,12},{5,13},{6,14},{7,15},{8,0},{9,1},... | collective-permute-start | bytes 6291464 | tf_op jit(solution)/shard_map/ppermute | solution.py:294
  290.8 80.9 %collective-permute-start.17 = (f32[2,16,128,128]{3,2,1,0:T(8,128)}, f32[2,16,128,128]{3,2,1,0:T(8,128)}, u32[]{:S(2)}, u32[]{:S(2)}) collective-permute-start(f32[2,16,128,128]{3,2,1,0:T(8,128)} %collective-permute-done.15.refs_7_), channel_id=1, source_target_pairs={{0,8},{1,9},{2,10},{3,11},{4,12},{5,13},{6,14},{7,15},{8,0},{9,1},... | collective-permute-start | bytes 6291464 | tf_op jit(solution)/shard_map/ppermute | solution.py:294
  290.8 80.9 %collective-permute-start.18 = (f32[2,16,128,128]{3,2,1,0:T(8,128)}, f32[2,16,128,128]{3,2,1,0:T(8,128)}, u32[]{:S(2)}, u32[]{:S(2)}) collective-permute-start(f32[2,16,128,128]{3,2,1,0:T(8,128)} %collective-permute-done.16.refs_8_), channel_id=1, source_target_pairs={{0,8},{1,9},{2,10},{3,11},{4,12},{5,13},{6,14},{7,15},{8,0},{9,1},... | collective-permute-start | bytes 6291464 | tf_op jit(solution)/shard_map/ppermute | solution.py:294
  324.8 82.6 %collective-permute-start.13 = (f32[2,16,128,128]{3,2,1,0:T(8,128)}, f32[2,16,128,128]{3,2,1,0:T(8,128)S(1)}, u32[]{:S(2)}, u32[]{:S(2)}) collective-permute-start(f32[2,16,128,128]{3,2,1,0:T(8,128)} %collective-permute-done.10.refs_7_), channel_id=1, source_target_pairs={{0,8},{1,9},{2,10},{3,11},{4,12},{5,13},{6,14},{7,15},{8,0},{9,1},... | collective-permute-start | bytes 6291464 | tf_op jit(solution)/shard_map/ppermute | solution.py:294
  338.0 69.4 %collective-permute-start.14 = (f32[2,16,128,128]{3,2,1,0:T(8,128)}, f32[2,16,128,128]{3,2,1,0:T(8,128)}, u32[]{:S(2)}, u32[]{:S(2)}) collective-permute-start(f32[2,16,128,128]{3,2,1,0:T(8,128)} %collective-permute-done.12.refs_8_), channel_id=1, source_target_pairs={{0,8},{1,9},{2,10},{3,11},{4,12},{5,13},{6,14},{7,15},{8,0},{9,1},... | collective-permute-start | bytes 6291464 | tf_op jit(solution)/shard_map/ppermute | solution.py:294
  407.3 1.3 copy-start.13
  443.8 12.5 %collective-permute-start.24 = (f32[32,128,128]{2,1,0:T(8,128)}, f32[32,128,128]{2,1,0:T(8,128)S(1)}, u32[]{:S(2)}, u32[]{:S(2)}) collective-permute-start(f32[32,128,128]{2,1,0:T(8,128)} %get-tuple-element.36), channel_id=1, source_target_pairs={{6,4},{7,5},{14,12},{15,13},{22,20},{23,21},{30,28},{31,29}} | collective-permute-start | bytes 6291464 | tf_op jit(solution)/shard_map/ppermute | solution.py:294
  444.6 53.0 %collective-permute-start.27 = (f32[32,128,128]{2,1,0:T(8,128)}, f32[32,128,128]{2,1,0:T(8,128)S(1)}, u32[]{:S(2)}, u32[]{:S(2)}) collective-permute-start(f32[32,128,128]{2,1,0:T(8,128)} %get-tuple-element.34), channel_id=1, source_target_pairs={{0,2},{1,3},{8,10},{9,11},{16,18},{17,19},{24,26},{25,27}} | collective-permute-start | bytes 6291464 | tf_op jit(solution)/shard_map/ppermute | solution.py:294
  497.6 8.3 %copy-start.1 = (f32[32,128,128]{2,1,0:T(8,128)S(1)}, f32[32,128,128]{2,1,0:T(8,128)}, u32[]{:S(2)}) copy-start(f32[32,128,128]{2,1,0:T(8,128)} %get-tuple-element.34) | copy-start | bytes 6291460
  500.1 5.9 collective-permute-start.25
  500.9 45.2 %copy-start = (f32[32,128,128]{2,1,0:T(8,128)S(1)}, f32[32,128,128]{2,1,0:T(8,128)}, u32[]{:S(2)}) copy-start(f32[32,128,128]{2,1,0:T(8,128)} %get-tuple-element.36) | copy-start | bytes 6291460
  500.9 45.2 %collective-permute-start.28 = (f32[32,128,128]{2,1,0:T(8,128)S(1)}, f32[32,128,128]{2,1,0:T(8,128)S(1)}, u32[]{:S(2)}, u32[]{:S(2)}) collective-permute-start(f32[32,128,128]{2,1,0:T(8,128)S(1)} %get-tuple-element.42), channel_id=1, source_target_pairs={{0,2},{1,3},{2,4},{3,5},{8,10},{9,11},{10,12},{11,13},{16,18},{17,... | collective-permute-start | bytes 6291464 | tf_op jit(solution)/shard_map/ppermute | solution.py:294
  506.3 105.8 %copy-start.5 = (f32[32,128,128]{2,1,0:T(8,128)S(1)}, f32[32,128,128]{2,1,0:T(8,128)}, u32[]{:S(2)}) copy-start(f32[32,128,128]{2,1,0:T(8,128)} %get-tuple-element.33) | copy-start | bytes 6291460
  506.3 103.8 %collective-permute-start.26 = (f32[32,128,128]{2,1,0:T(8,128)S(1)}, f32[32,128,128]{2,1,0:T(8,128)S(1)}, u32[]{:S(2)}, u32[]{:S(2)}) collective-permute-start(f32[32,128,128]{2,1,0:T(8,128)S(1)} %add.331), channel_id=1, source_target_pairs={{2,0},{3,1},{4,2},{5,3},{6,4},{7,5},{10,8},{11,9},{12,10},{13,11},... | collective-permute-start | bytes 6291464 | tf_op jit(solution)/shard_map/ppermute | solution.py:294
  546.3 65.8 %collective-permute-start.29 = (f32[32,128,128]{2,1,0:T(8,128)S(1)}, f32[32,128,128]{2,1,0:T(8,128)S(1)}, u32[]{:S(2)}, u32[]{:S(2)}) collective-permute-start(f32[32,128,128]{2,1,0:T(8,128)S(1)} %add.334), channel_id=1, source_target_pairs={{0,2},{1,3},{2,4},{3,5},{4,6},{5,7},{8,10},{9,11},{10,12},{11,13},... | collective-permute-start | bytes 6291464 | tf_op jit(solution)/shard_map/ppermute | solution.py:294
  613.0 7.2 %collective-permute-start.30 = (f32[16,128,128]{2,1,0:T(8,128)S(1)}, f32[16,128,128]{2,1,0:T(8,128)S(1)}, u32[]{:S(2)}, u32[]{:S(2)}) collective-permute-start(f32[16,128,128]{2,1,0:T(8,128)S(1)} %get-tuple-element.39), channel_id=1, source_target_pairs={{0,0},{1,8},{2,2},{3,10},{4,4},{5,12},{6,6},{7,14},{8,1},{9,9},{10... | collective-permute-start | bytes 3145736 | tf_op jit(solution)/shard_map/ppermute | solution.py:294
  613.7 29.4 %collective-permute-start.31 = (f32[16,128,128]{2,1,0:T(8,128)S(1)}, f32[16,128,128]{2,1,0:T(8,128)}, u32[]{:S(2)}, u32[]{:S(2)}) collective-permute-start(f32[16,128,128]{2,1,0:T(8,128)S(1)} %get-tuple-element.40), channel_id=1, source_target_pairs={{0,1},{1,9},{2,3},{3,11},{4,5},{5,13},{6,7},{7,15},{8,0},{9,8},{10... | collective-permute-start | bytes 3145736 | tf_op jit(solution)/shard_map/ppermute | solution.py:294
